TPU v7x, 32 devices: a whole 2x2x4 slice. The times are simulated.
32 devices in a mesh: prow: 4 (over y, x), pcol: 8 (over z, core).
Axes of the slice: x: 2, y: 2, z: 4, core: 2. Of those that a mesh axis runs over, the one named last changes fastest.
Arguments:
- matrix: float32 [2048, 1024], P('prow', 'pcol'), may hold values from -6 to 6
- panel: float32 [2048, 1024], P(('prow', 'pcol')), as said below
- pivots: int32 [1024], replicated, may hold values from 0 to 2047, as said below
Outputs:
- trailing: float32 [2048, 1024], P('prow', 'pcol')
Inputs may be any that keep to these rules, and one draw needn't show every extreme that they name: pivots[i] is either i itself or a row at or beyond 1024; the rows at or beyond 1024 that are named are all different; at most 264 of them lie in the rows of one index of prow, and some index of prow holds exactly 264. `panel`: the top 1024 rows are unit lower triangular.
All inputs are finite; a program needn't handle non-finite values.
Results may differ from a plain program's by a relative error of at most 0.000061.
Values sent between devices are 32-bit elements; how exact they have to be, the bound alone decides.
No kernel may reach another device: no remote copies, remote signals or barrier semaphores. Data moves between devices by JAX's collectives and lax.ppermute only.
A program may use at most 64 MiB of HBM per device.

v0:
```python
import jax
import jax.numpy as jnp
from jax import lax
from jax.sharding import PartitionSpec as P


def spread(block, axis, holder):
    block = jnp.where(lax.axis_index(axis) == holder, block, jnp.zeros_like(block))
    return lax.psum(block, axis)


def per_device(matrix, panel, pivots):
    rows, cols = matrix.shape
    block = pivots.shape[0]
    first = lax.axis_index("prow") * rows
    local_pivot = pivots - first
    owned = (local_pivot >= 0) & (local_pivot < rows)
    picked = jnp.take(matrix, jnp.clip(local_pivot, 0, rows - 1), axis=0)
    picked = jnp.where(owned[:, None], picked, 0.0)
    panel_block = lax.all_gather(panel, "pcol", axis=0, tiled=True)
    shares = lax.psum_scatter(picked, "prow", scatter_dimension=0, tiled=True)
    solved = jnp.dot(
        panel_block,
        lax.all_gather(shares, "prow", axis=0, tiled=True),
        precision=lax.Precision.HIGHEST,
        preferred_element_type=jnp.float32,
    )
    rows_here = first + jnp.arange(rows, dtype=jnp.int32)
    match = pivots[None, :] == rows_here[:, None]
    moved = jnp.any(match, axis=1) & (rows_here >= block)
    source = jnp.sum(jnp.where(match, jnp.arange(block, dtype=jnp.int32)[None, :], 0), axis=1)
    upper = jnp.zeros((block, cols), jnp.float32)
    top_old = jnp.zeros((block, cols), jnp.float32)
    for root in range(block // rows):
        piece_u, old_rows = (spread(solved, "prow", root), spread(matrix, "prow", root))
        upper = lax.dynamic_update_slice_in_dim(upper, piece_u, root * rows, 0)
        top_old = lax.dynamic_update_slice_in_dim(top_old, old_rows, root * rows, 0)
    replaced = jnp.take(top_old, source, axis=0)
    permuted = jnp.where(moved[:, None], replaced, matrix)
    lower = permuted - jnp.dot(
        panel_block, upper, precision=lax.Precision.HIGHEST, preferred_element_type=jnp.float32
    )
    return jnp.where((rows_here < block)[:, None], solved, lower)


def solution(mesh):
    placed = (P("prow", "pcol"), P(("prow", "pcol"), None), P())
    return jax.shard_map(
        per_device, mesh=mesh, in_specs=placed, out_specs=P("prow", "pcol"), check_vma=False
    )
```

profile of v0, /device:TPU:0, one launch (start us, length us, event | category | flops | bytes accessed | tf_op | source)
XLA Modules:
  0.0 123.5 jit_solution(4456176629479633744)
XLA Ops:
  7.4 0.0 reduce-scatter.2.cloned.1.call-start
  7.4 0.7 fusion.6
  8.1 0.7 compare_and_fusion.1
  8.8 0.0 copy-start
  8.8 3.8 %gather_fusion = f32[1024,128]{1,0:T(8,128)S(1)} fusion(f32[512,128]{1,0:T(8,128)} %param.3, s32[1024]{0:T(1024)S(1)} %fusion.6), kind=kCustom, calls=%fused_computation | custom fusion | bytes 1052672 | tf_op jit(solution)/shard_map/jit(_take)/gather | solution.py:18
  12.6 1.1 select_select_fusion
  13.7 0.0 reduce-scatter.2.cloned.1.call-update
  13.8 0.0 all-gather.2.cloned.1.call-start
  13.8 0.5 all-gather.2.cloned.1.call-update
  14.3 0.0 all-reduce.3.cloned.1.call-start
  14.4 0.0 copy-done
  14.4 0.1 copy.16
  14.5 0.9 broadcast_select_fusion.3
  15.4 26.3 %reduce-scatter.2.cloned.1.call-done = f32[256,128]{1,0:T(8,128)} async-done(((f32[1024,128]{1,0:T(8,128)}), f32[256,128]{1,0:T(8,128)}) %reduce-scatter.2.cloned.1.call-update) | async-done | bytes 131088 | tf_op jit(solution)/shard_map/reduce_scatter | solution.py:21
  41.7 10.0 %all_gather.6 = f32[1024,128]{1,0:T(8,128)S(1)} all-gather(f32[256,128]{1,0:T(8,128)} %reduce-scatter.2.cloned.1.call-done), channel_id=1, replica_groups=mesh['prow'=4,'pcol'=8] {'prow'}, dimensions={0}, use_global_device_ids=true | all-gather | bytes 655360 | tf_op jit(solution)/shard_map/all_gather | solution.py:24
  51.7 0.0 copy-start.3
  51.7 0.0 all-gather.2.cloned.1.call-done
  51.8 4.8 %broadcast_select_fusion.1 = (f32[512,128]{0,1:T(8,128)}, f32[512,128]{0,1:T(8,128)}, f32[512,128]{0,1:T(8,128)}) fusion(pred[]{:T(512)S(6)} %eq.24, pred[]{:T(512)S(6)} %eq.25, f32[1024,128]{1,0:T(8,128)S(1)} %all_gather.6, f32[512,1024]{1,0:T(8,128)} %all-gather.2.cloned.1.call-done), kind=kOutput, calls=%fused_computation.15 | convolution fusion | flops 805437440 | bytes 3407874 | tf_op jit(solution)/shard_map/dot_general | solution.py:22
  56.5 0.0 all-reduce.3.cloned.1.call-update
  56.6 0.0 copy-done.3
  56.6 0.4 fusion
  57.0 0.4 compare_reduce_fusion
  57.4 51.8 %all-reduce.3.cloned.1.call-done = (f32[512,128]{0,1:T(8,128)}, f32[512,128]{0,1:T(8,128)}, f32[512,128]{0,1:T(8,128)}, f32[512,128]{0,1:T(8,128)}) async-done(((f32[512,128]{0,1:T(8,128)}, f32[512,128]{0,1:T(8,128)}, f32[512,128]{0,1:T(8,128)}, f32[512,128]{0,1:T(8,128)}), (f32[512,128]{0,1:T(8,128)}, f32[512,128]{0,1:T(8,128)}, f32[512,128]{0,1:T(8,128)}, ...) | async-done | bytes 1048592 | tf_op jit(solution)/shard_map/psum | solution.py:9
  109.3 1.1 pad_maximum_fusion
  110.3 0.0 copy-start.1
  110.3 0.2 copy.18
  110.5 0.0 copy-start.2
  110.5 1.0 gather_fusion.1
  111.6 0.1 copy.19
  111.7 0.2 copy-done.1
  111.9 0.0 copy-done.2
  111.9 3.3 %fusion.2 = f32[512,128]{0,1:T(8,128)S(1)} fusion(f32[512,128]{0,1:T(8,128)S(1)} %copy-done.2, f32[512,1024]{1,0:T(8,128)S(1)} %copy-done.1, f32[512,128]{0,1:T(8,128)} %get-tuple-element.5, f32[512,128]{0,1:T(8,128)} %get-tuple-element.6, f32[512,128]{0,1:T(8,128)S(1)} %copy.16, f32[512,128]{0,1:T(8,128)S(1)} %copy.19, ...), kind=kOutput, calls=%fused_computation.8 | convolution fusion | flops 805699584 | bytes 3671552 | tf_op jit(solution)/shard_map/dot_general | solution.py:40
  115.2 0.8 copy.21
  (5 shorter events, 0.0 us)
Async XLA Ops:
  7.4 34.4 %reduce-scatter.2.cloned.1.call-start = ((), (), s32[]{:S(2)}) async-start(), calls=%async_computation.1 | async-start | bytes 655360 | tf_op jit(solution)/shard_map/reduce_scatter | solution.py:21
  8.8 5.6 %copy-start = (f32[512,128]{1,0:T(8,128)S(1)}, f32[512,128]{1,0:T(8,128)}, u32[]{:S(2)}) copy-start(f32[512,128]{1,0:T(8,128)} %param.3) | copy-start | bytes 786436
  13.8 38.0 %all-gather.2.cloned.1.call-start = ((), (), s32[]{:S(2)}) async-start(), calls=%async_computation.2 | async-start | bytes 2359296 | tf_op jit(solution)/shard_map/all_gather | solution.py:20
  14.3 94.9 %all-reduce.3.cloned.1.call-start = ((), (), s32[]{:S(2)}) async-start(), calls=%async_computation.3 | async-start | bytes 2097152 | tf_op jit(solution)/shard_map/psum | solution.py:9
  51.7 4.9 %copy-start.3 = (s32[1024]{0:T(1024)S(1)}, s32[1024]{0:T(1024)}, u32[]{:S(2)}) copy-start(s32[1024]{0:T(1024)} %param.5) | copy-start | bytes 12292
  110.3 1.6 %copy-start.1 = (f32[512,1024]{1,0:T(8,128)S(1)}, f32[512,1024]{1,0:T(8,128)}, u32[]{:S(2)}) copy-start(f32[512,1024]{1,0:T(8,128)} %all-gather.2.cloned.1.call-done) | copy-start | bytes 6291460
  110.5 1.4 %copy-start.2 = (f32[512,128]{0,1:T(8,128)S(1)}, f32[512,128]{0,1:T(8,128)}, u32[]{:S(2)}) copy-start(f32[512,128]{0,1:T(8,128)} %get-tuple-element.15) | copy-start | bytes 786436
Sparse Core Ops, SparseCore 0:
  13.9 27.8 reduce-scatter.1
  56.7 52.5 all-reduce.2
Sparse Core Ops, SparseCore 1:
  15.8 31.8 all-gather.1
where the time goes:
time: 124 us; the launch traced here: 123 us
  waiting for transfers between devices  78.7 us (63%)
  between operations  15 us (12%)
  blocking collectives  9.99 us (8%)
  matrix products  8.06 us (6%)
  local copies, waits for them, and re-layouts  6.37 us (5%)
  other arithmetic  5.29 us (4%)
    psum x1, waiting for transfers between devices, spread(): return lax.psum(block, axis)  51.8 us
    reduce_scatter x1, waiting for transfers between devices, per_device(): shares = lax.psum_scatter(picked, 'prow', scatter_dimension=0, tiled=True)  26.3 us
    all_gather x1, blocking collectives, per_device(): lax.all_gather(shares, 'prow', axis=0, tiled=True)  9.99 us
    dot_general x1, matrix products, per_device(): jnp.dot(panel_block, lax.all_gather(shares, 'prow', axis=0, tiled=True),...  4.79 us
    gather x1, local copies, waits for them, and re-layouts, per_device(): picked = jnp.take(matrix, jnp.clip(local_pivot, 0, rows - 1), axis=0)  3.82 us
    dot_general x1, matrix products, per_device(): jnp.dot(panel_block, upper, precision=lax.Precision.HIGHEST, preferred_el...  3.28 us
  transfers between devices with their start and end apart: 3, of which 2 were waited for; matrix products, arithmetic and copies ran while one was open for 1% of the time, Pallas kernels for 0%

commit v1 on v0

--- a/solution.py
+++ b/solution.py
@@ -4,9 +4,15 @@
 from jax.sharding import PartitionSpec as P
 
 
+def add_all(x, mesh_axis):
+    parts = lax.all_gather(x, mesh_axis, axis=0, tiled=False)
+    total = parts.sum(axis=0)
+    return total
+
+
 def spread(block, axis, holder):
     block = jnp.where(lax.axis_index(axis) == holder, block, jnp.zeros_like(block))
-    return lax.psum(block, axis)
+    return add_all(block, axis)
 
 
 def per_device(matrix, panel, pivots):

time: 124 us -> 175 us (1.41)
  waiting for transfers between devices: 78.7 us -> 118 us
  local copies, waits for them, and re-layouts: 6.37 us -> 14.7 us
  other arithmetic: 5.29 us -> 8.16 us
    all_gather x0 -> x4, waiting for transfers between devices: none -> 91 us  [add_all(): parts = lax.all_gather(x, mesh_axis, axis=0, tiled=False)]
    psum x1 -> x0, waiting for transfers between devices: 51.8 us -> none  [spread(): return lax.psum(block, axis)]
    all_gather x0 -> x4, local copies, waits for them, and re-layouts: none -> 7.73 us  [add_all(): parts = lax.all_gather(x, mesh_axis, axis=0, tiled=False)]
    reduce_sum x0 -> x4, other arithmetic: none -> 3.91 us  [add_all(): total = parts.sum(axis=0)]
  transfers between devices with their start and end apart: 3 -> 6, of which waited for: 2 -> 5; matrix products, arithmetic and copies ran while one was open for 1% -> 10% of each run, Pallas kernels for 0% -> 0%
where the time goes in v1:
time: 175 us
  waiting for transfers between devices  118 us (67%)
  between operations  15.2 us (9%)
  local copies, waits for them, and re-layouts  14.7 us (8%)
  blocking collectives  9.99 us (6%)
  matrix products  8.24 us (5%)
  other arithmetic  8.16 us (5%)
    all_gather x4, waiting for transfers between devices, add_all(): parts = lax.all_gather(x, mesh_axis, axis=0, tiled=False)  91 us
    reduce_scatter x1, waiting for transfers between devices, per_device(): shares = lax.psum_scatter(picked, 'prow', scatter_dimension=0, tiled=True)  25.7 us
    all_gather x1, blocking collectives, per_device(): lax.all_gather(shares, 'prow', axis=0, tiled=True)  9.99 us
    all_gather x4, local copies, waits for them, and re-layouts, add_all(): parts = lax.all_gather(x, mesh_axis, axis=0, tiled=False)  7.73 us
    dot_general x1, matrix products, per_device(): jnp.dot(panel_block, lax.all_gather(shares, 'prow', axis=0, tiled=True),...  4.81 us
    reduce_sum x4, other arithmetic, add_all(): total = parts.sum(axis=0)  3.91 us
    gather x1, local copies, waits for them, and re-layouts, per_device(): picked = jnp.take(matrix, jnp.clip(local_pivot, 0, rows - 1), axis=0)  3.82 us
  transfers between devices with their start and end apart: 6, of which 5 were waited for; matrix products, arithmetic and copies ran while one was open for 10% of the time, Pallas kernels for 0%

profile of v1, /device:TPU:0, one launch (start us, length us, event | category | flops | bytes accessed | tf_op | source)
XLA Modules:
  0.0 175.0 jit_solution(6339947585957251605)
XLA Ops:
  7.4 0.0 reduce-scatter.2.cloned.1.call-start
  7.4 0.7 compare_and_fusion.1
  8.1 0.7 fusion.6
  8.8 0.0 copy-start
  8.8 3.8 %gather_fusion = f32[1024,128]{1,0:T(8,128)S(1)} fusion(f32[512,128]{1,0:T(8,128)} %param.3, s32[1024]{0:T(1024)S(1)} %fusion.6), kind=kCustom, calls=%fused_computation | custom fusion | bytes 1052672 | tf_op jit(solution)/shard_map/jit(_take)/gather | solution.py:24
  12.6 1.1 select_select_fusion
  13.7 0.0 reduce-scatter.2.cloned.1.call-update
  13.8 0.0 all-gather.10.cloned.1.call-start
  13.8 0.5 all-gather.10.cloned.1.call-update
  14.3 0.0 all-gather.12.cloned.1.call-start
  14.4 0.0 copy-done
  14.4 0.1 copy.21
  14.5 0.9 broadcast_select_fusion.3
  15.4 0.0 all-gather.12.cloned.1.call-update
  15.4 0.0 all-gather.14.cloned.1.call-start
  15.5 0.5 all-gather.14.cloned.1.call-update
  16.0 0.0 all-gather.16.cloned.1.call-start
  16.1 25.7 %reduce-scatter.2.cloned.1.call-done = f32[256,128]{1,0:T(8,128)} async-done(((f32[1024,128]{1,0:T(8,128)}), f32[256,128]{1,0:T(8,128)}) %reduce-scatter.2.cloned.1.call-update) | async-done | bytes 131088 | tf_op jit(solution)/shard_map/reduce_scatter | solution.py:27
  41.7 10.0 %all_gather.30 = f32[1024,128]{1,0:T(8,128)S(1)} all-gather(f32[256,128]{1,0:T(8,128)} %reduce-scatter.2.cloned.1.call-done), channel_id=1, replica_groups=mesh['prow'=4,'pcol'=8] {'prow'}, dimensions={0}, use_global_device_ids=true | all-gather | bytes 655360 | tf_op jit(solution)/shard_map/all_gather | solution.py:30
  51.7 0.0 copy-start.2
  51.7 0.0 all-gather.10.cloned.1.call-done
  51.8 4.8 %broadcast_select_fusion.1 = (f32[512,128]{0,1:T(8,128)}, f32[512,128]{0,1:T(8,128)}, f32[512,128]{0,1:T(8,128)}) fusion(pred[]{:T(512)S(6)} %eq.24, pred[]{:T(512)S(6)} %eq.25, f32[1024,128]{1,0:T(8,128)S(1)} %all_gather.30, f32[512,1024]{1,0:T(8,128)} %all-gather.10.cloned.1.call-done), kind=kOutput, calls=%fused_computation.15 | convolution fusion | flops 805437440 | bytes 3407874 | tf_op jit(solution)/shard_map/dot_general | solution.py:28
  56.6 0.0 all-gather.16.cloned.1.call-update
  56.6 0.2 all-gather.18.cloned.1.call-start
  56.8 0.5 all-gather.18.cloned.1.call-update
  57.4 0.0 copy-done.2
  57.4 0.4 fusion
  57.8 0.4 compare_reduce_fusion
  58.2 16.9 %all-gather.12.cloned.1.call-done = f32[2048,128]{0,1:T(8,128)} async-done(((f32[512,128]{0,1:T(8,128)}), f32[2048,128]{0,1:T(8,128)}) %all-gather.12.cloned.1.call-update) | async-done | bytes 1048592 | tf_op jit(solution)/shard_map/all_gather | solution.py:8
  75.2 1.9 %reshape.54 = f32[4,512,128]{1,0,2:T(4,128)S(1)} reshape(f32[2048,128]{0,1:T(8,128)} %all-gather.12.cloned.1.call-done) | data formatting | bytes 2097152 | tf_op jit(solution)/shard_map/all_gather | solution.py:8
  77.1 0.6 reduce_sum.48
  77.7 0.1 copy.23
  77.9 25.4 %all-gather.14.cloned.1.call-done = f32[2048,128]{0,1:T(8,128)} async-done(((f32[512,128]{0,1:T(8,128)}), f32[2048,128]{0,1:T(8,128)}) %all-gather.14.cloned.1.call-update) | async-done | bytes 1048592 | tf_op jit(solution)/shard_map/all_gather | solution.py:8
  103.3 1.9 %reshape.55 = f32[4,512,128]{1,0,2:T(4,128)S(1)} reshape(f32[2048,128]{0,1:T(8,128)} %all-gather.14.cloned.1.call-done) | data formatting | bytes 2097152 | tf_op jit(solution)/shard_map/all_gather | solution.py:8
  105.2 0.6 reduce_sum.49
  105.9 0.1 copy.24
  106.0 1.0 gather_fusion.1
  107.1 0.9 copy.25
  107.9 23.6 %all-gather.16.cloned.1.call-done = f32[2048,128]{0,1:T(8,128)} async-done(((f32[512,128]{0,1:T(8,128)}), f32[2048,128]{0,1:T(8,128)}) %all-gather.16.cloned.1.call-update) | async-done | bytes 1048592 | tf_op jit(solution)/shard_map/all_gather | solution.py:8
  131.6 1.9 %reshape.56 = f32[4,512,128]{1,0,2:T(4,128)S(1)} reshape(f32[2048,128]{0,1:T(8,128)} %all-gather.16.cloned.1.call-done) | data formatting | bytes 2097152 | tf_op jit(solution)/shard_map/all_gather | solution.py:8
  133.5 0.0 copy-start.1
  133.5 1.3 reduce_sum.51
  134.8 25.0 %all-gather.18.cloned.1.call-done = f32[2048,128]{0,1:T(8,128)} async-done(((f32[512,128]{0,1:T(8,128)}), f32[2048,128]{0,1:T(8,128)}) %all-gather.18.cloned.1.call-update) | async-done | bytes 1048592 | tf_op jit(solution)/shard_map/all_gather | solution.py:8
  159.8 1.9 %reshape.57 = f32[4,512,128]{1,0,2:T(4,128)S(1)} reshape(f32[2048,128]{0,1:T(8,128)} %all-gather.18.cloned.1.call-done) | data formatting | bytes 2097152 | tf_op jit(solution)/shard_map/all_gather | solution.py:8
  161.8 1.3 reduce_sum.52
  163.1 0.0 copy-done.1
  163.1 3.4 %fusion.2 = f32[512,128]{0,1:T(8,128)S(1)} fusion(f32[512,128]{0,1:T(8,128)} %get-tuple-element.11, f32[512,1024]{1,0:T(8,128)S(1)} %copy-done.1, f32[512,128]{0,1:T(8,128)} %reduce_sum.52, f32[512,128]{0,1:T(8,128)} %reduce_sum.51, f32[512,128]{0,1:T(8,128)S(1)} %copy.21, f32[512,128]{0,1:T(8,128)} %copy.25, pred[512]{0:T(512)(128)(4,1)S(1)} %compare_and_fusion.2, ...), kind=kOutput, calls=%fused_computation.8 | convolution fusion | flops 805699584 | bytes 3671552 | tf_op jit(solution)/shard_map/dot_general | solution.py:46
  166.6 0.8 copy.27
  (7 shorter events, 0.1 us)
Async XLA Ops:
  7.4 34.4 %reduce-scatter.2.cloned.1.call-start = ((), (), s32[]{:S(2)}) async-start(), calls=%async_computation.1 | async-start | bytes 655360 | tf_op jit(solution)/shard_map/reduce_scatter | solution.py:27
  8.8 5.6 %copy-start = (f32[512,128]{1,0:T(8,128)S(1)}, f32[512,128]{1,0:T(8,128)}, u32[]{:S(2)}) copy-start(f32[512,128]{1,0:T(8,128)} %param.3) | copy-start | bytes 786436
  13.8 38.0 %all-gather.10.cloned.1.call-start = ((), (), s32[]{:S(2)}) async-start(), calls=%async_computation.2 | async-start | bytes 2359296 | tf_op jit(solution)/shard_map/all_gather | solution.py:26
  14.3 60.8 %all-gather.12.cloned.1.call-start = ((), (), s32[]{:S(2)}) async-start(), calls=%async_computation.3 | async-start | bytes 1310720 | tf_op jit(solution)/shard_map/all_gather | solution.py:8
  15.4 87.9 %all-gather.14.cloned.1.call-start = ((), (), s32[]{:S(2)}) async-start(), calls=%async_computation.4 | async-start | bytes 1310720 | tf_op jit(solution)/shard_map/all_gather | solution.py:8
  16.0 115.6 %all-gather.16.cloned.1.call-start = ((), (), s32[]{:S(2)}) async-start(), calls=%async_computation.5 | async-start | bytes 1310720 | tf_op jit(solution)/shard_map/all_gather | solution.py:8
  51.7 5.6 %copy-start.2 = (s32[1024]{0:T(1024)S(1)}, s32[1024]{0:T(1024)}, u32[]{:S(2)}) copy-start(s32[1024]{0:T(1024)} %param.5) | copy-start | bytes 12292
  56.6 103.3 %all-gather.18.cloned.1.call-start = ((), (), s32[]{:S(2)}) async-start(), calls=%async_computation.6 | async-start | bytes 1310720 | tf_op jit(solution)/shard_map/all_gather | solution.py:8
  133.5 29.6 %copy-start.1 = (f32[512,1024]{1,0:T(8,128)S(1)}, f32[512,1024]{1,0:T(8,128)}, u32[]{:S(2)}) copy-start(f32[512,1024]{1,0:T(8,128)} %all-gather.10.cloned.1.call-done) | copy-start | bytes 6291460
Sparse Core Ops, SparseCore 0:
  13.9 27.8 reduce-scatter.1
Sparse Core Ops, SparseCore 1:
  15.8 31.8 all-gather.9
  49.4 25.7 all-gather.11
  76.9 26.3 all-gather.13
  105.2 26.3 all-gather.15
  133.4 26.3 all-gather.17
